TPU v7x, 512 devices: a whole 4x8x8 slice. The times are simulated.
512 devices in a mesh: blk: 8 (over z_hi, core), win: 64 (over x, y, z_lo).
Axes of the slice: x: 4, y: 8, z: 8 (z_hi: 4, z_lo: 2; z = z_hi * 2 + z_lo), core: 2. Of those that a mesh axis runs over, the one named last changes fastest.
Arguments:
- frame_tokens: bfloat16 [8, 64, 128, 1024], P('blk', 'win'), may hold values from -21 to 21, as said below
- w_kv: bfloat16 [1024, 2048], replicated, may hold values from -0.1875 to 0.1875
- w_q: bfloat16 [1024, 1024], P('win'), may hold values from -0.1875 to 0.1875
- w_out: bfloat16 [1024, 1024], P('win'), may hold values from -0.1875 to 0.1875
- slot_tokens: int32 [8, 64, 128], P(None, 'win'), may hold values from 0 to 1023, as said below
- counts: int32 [8, 64], P('blk', 'win'), may hold values from 32 to 128, as said below
Outputs:
- projected: bfloat16 [8, 64, 128, 1024], P('blk', 'win')
Inputs may be any that keep to these rules, and one draw needn't show every extreme that they name: `frame_tokens`: shown draw: a normal law truncated at 6. `slot_tokens`: every slot names a token of its own window. For each frame group and window the 128 slots name tokens of exactly 4 frames, 32 from each; no token of a window is named twice. `counts`: slots below the count are live. Each window has a frame group with all 128 slots live.
All inputs are finite; a program needn't handle non-finite values.
Results may differ from a plain program's by a relative error of at most 0.012.
The roundings to bfloat16 on the way count: a program that leaves them out, or rounds other values in their place, can miss the bound.
Values may be sent and summed in bfloat16 or wider, within the bound.
A program may use at most 64 MiB of HBM per device.

v0:
```python
import jax
import jax.numpy as jnp
from jax import lax
from jax.sharding import PartitionSpec as P

HEADS = 16


def add_rows(left_rows, shard_rows):
    return jnp.dot(left_rows, shard_rows, preferred_element_type=jnp.float32)


def absorb(state_now, key_rows, value_rows, query_heads, score_scale):
    row_peak, total_sum, accum_rows = state_now
    win_dev, slot_count, head_count, head_dim = query_heads.shape
    key_heads = key_rows.reshape(win_dev, -1, head_count, head_dim)
    value_heads = value_rows.reshape(win_dev, -1, head_count, head_dim)
    scores = (
        jnp.einsum("jshd,jkhd->jhsk", query_heads, key_heads, preferred_element_type=jnp.float32)
        * score_scale
    )
    new_peak = jnp.maximum(row_peak, jnp.max(scores, axis=-1))
    raw_weights = jnp.exp(scores - new_peak[..., None])
    total_sum = jnp.sum(raw_weights, axis=-1)
    mixed_rows = jnp.einsum(
        "jhsk,jkhd->jshd",
        raw_weights.astype(jnp.bfloat16),
        value_heads,
        preferred_element_type=jnp.float32,
    )
    accum_rows = mixed_rows
    return (new_peak, total_sum, accum_rows)


def local(frame_tokens, w_kv, w_q, w_out, slot_tokens, counts):
    groups = lax.axis_size("blk")
    group_at = lax.axis_index("blk")
    frames_here, win_dev, window_len, model_width = frame_tokens.shape
    slot_count = slot_tokens.shape[2]
    per_owner = slot_count // min(4, groups)
    head_count = HEADS
    head_dim = model_width // head_count
    score_scale = head_dim ** (-0.5)
    frame_rows = frame_tokens[0]
    source_group = slot_tokens // window_len
    is_mine = source_group == group_at
    mine_count = is_mine.astype(jnp.int32)
    rank_of = jnp.cumsum(mine_count, axis=-1) - mine_count
    place_at = jnp.where(is_mine, rank_of, per_owner)
    slot_onehot = (place_at[..., None] == jnp.arange(per_owner, dtype=jnp.int32)).astype(
        jnp.bfloat16
    )
    token_onehot = (
        (slot_tokens - group_at * window_len)[..., None] == jnp.arange(window_len, dtype=jnp.int32)
    ).astype(jnp.bfloat16)
    selector = jnp.einsum(
        "gjsc,gjsu->gjcu", slot_onehot, token_onehot, preferred_element_type=jnp.float32
    ).astype(jnp.bfloat16)
    outgoing = jnp.einsum(
        "gjcu,jud->jgcd", selector, frame_rows, preferred_element_type=jnp.float32
    ).astype(jnp.bfloat16)
    arrived = lax.all_to_all(outgoing, "blk", split_axis=1, concat_axis=1, tiled=True)
    incoming = arrived.reshape(win_dev, groups * per_owner, model_width)
    own_picks = lax.dynamic_index_in_dim(slot_tokens, group_at, 0, keepdims=False)
    own_source = own_picks // window_len
    hit_table = (own_source[..., None] == jnp.arange(groups, dtype=jnp.int32)).astype(jnp.int32)
    before = jnp.cumsum(hit_table, axis=1) - hit_table
    order_in = jnp.sum(before * hit_table, axis=-1)
    spot_at = own_source * per_owner + order_in
    grab_rows = (spot_at[..., None] == jnp.arange(groups * per_owner, dtype=jnp.int32)).astype(
        jnp.bfloat16
    )
    picked_rows = (
        jnp.einsum("jsr,jrd->jsd", grab_rows, incoming, preferred_element_type=jnp.float32)
        .astype(jnp.bfloat16)
        .reshape(-1, model_width)
    )
    query_flat = add_rows(picked_rows, lax.all_gather(w_q, "win", axis=0, tiled=True))
    query_heads = query_flat.astype(jnp.bfloat16).reshape(win_dev, slot_count, head_count, head_dim)
    initial = (
        jnp.full((win_dev, head_count, slot_count), -1e30, jnp.float32),
        jnp.zeros((win_dev, head_count, slot_count), jnp.float32),
        jnp.zeros((win_dev, slot_count, head_count, head_dim), jnp.float32),
    )
    key_value = jnp.einsum(
        "fjpd,de->jfpe",
        lax.all_gather(frame_tokens, "blk", axis=0, tiled=True),
        w_kv,
        preferred_element_type=jnp.float32,
    ).astype(jnp.bfloat16)
    key_value = key_value.reshape(win_dev, -1, 2 * model_width)
    state_end = absorb(
        initial,
        key_value[..., :model_width],
        key_value[..., model_width:],
        query_heads,
        score_scale,
    )
    final_peak, final_total, final_accum = state_end
    attended = (
        (final_accum / jnp.transpose(final_total, (0, 2, 1))[..., None])
        .astype(jnp.bfloat16)
        .reshape(-1, model_width)
    )
    out_sum = add_rows(attended, lax.all_gather(w_out, "win", axis=0, tiled=True))
    live_mask = (jnp.arange(slot_count, dtype=jnp.int32)[None, :] < counts[0][:, None]).astype(
        jnp.float32
    )
    return (
        (out_sum * live_mask.reshape(-1, 1))
        .astype(jnp.bfloat16)
        .reshape(1, win_dev, slot_count, model_width)
    )


def solution(mesh):
    placed = (
        P("blk", "win", None, None),
        P(),
        P("win", None),
        P("win", None),
        P(None, "win", None),
        P("blk", "win"),
    )
    return jax.shard_map(
        local, mesh=mesh, in_specs=placed, out_specs=P("blk", "win", None, None), check_vma=False
    )
```

profile of v0, /device:TPU:8, one launch (start us, length us, event | category | flops | bytes accessed | tf_op | source)
XLA Modules:
  0.0 670.5 jit_solution(2670747314636077683)
XLA Ops:
  6.5 0.0 all-gather.4.cloned.1.call-start
  6.5 0.7 all-gather.4.cloned.1.call-update
  7.3 0.0 all-gather.6.cloned.1.call-start
  7.3 0.7 all-gather.6.cloned.1.call-update
  8.0 0.7 fusion.39
  8.7 0.3 reduce_window_sum.23
  9.0 0.7 broadcast_subtract_fusion
  9.7 2.3 fusion.15
  12.0 10.3 %all-to-all-start = ((bf16[1,8,32,1024]{3,2,0,1:T(8,128)(2,1)}), bf16[1,8,32,1024]{3,2,0,1:T(8,128)(2,1)S(1)}, u32[]{:S(2)}, u32[]{:S(2)}) async-start(bf16[1,8,32,1024]{3,2,0,1:T(8,128)(2,1)} %fusion.15), calls=%async_computation | async-start | bytes 1048576 | tf_op jit(solution)/shard_map/all_to_all | solution.py:62
  22.3 0.0 all-gather.8.cloned.1.call-start
  22.3 0.7 all-gather.8.cloned.1.call-update
  23.0 0.7 and_select_fusion
  23.7 0.1 fusion.34
  23.8 0.2 reduce_window_sum.22
  24.6 0.2 select_reduce_fusion
  24.8 0.7 multiply_add_fusion
  25.5 30.7 %all-gather.4.cloned.1.call-done = bf16[8,1,128,1024]{3,2,1,0:T(8,128)(2,1)} async-done(((bf16[1,1,128,1024]{3,2,1,0:T(8,128)(2,1)}), bf16[8,1,128,1024]{3,2,1,0:T(8,128)(2,1)}) %all-gather.4.cloned.1.call-update) | async-done | bytes 2097168 | tf_op jit(solution)/shard_map/all_gather | solution.py:87
  56.2 7.4 %fusion.8 = bf16[2048,8,128]{0,2,1:T(8,128)(2,1)S(1)} fusion(bf16[1024,2048]{1,0:T(8,128)(2,1)} %param.7, bf16[8,1,128,1024]{3,2,1,0:T(8,128)(2,1)} %all-gather.4.cloned.1.call-done), kind=kOutput, calls=%fused_computation.9 | convolution fusion | flops 4297064448 | bytes 10485760 | tf_op jit(solution)/shard_map/fjpd,de->jfpe/dot_general | solution.py:85
  63.6 1.8 fusion.41
  65.4 2.6 copy.23
  67.9 2.9 copy.30
  70.8 0.0 all-to-all-done
  70.8 289.0 %all-gather.6.cloned.1.call-done = bf16[1024,1024]{1,0:T(8,128)(2,1)} async-done(((bf16[16,1024]{1,0:T(8,128)(2,1)}), bf16[1024,1024]{1,0:T(8,128)(2,1)}) %all-gather.6.cloned.1.call-update) | async-done | bytes 2097168 | tf_op jit(solution)/shard_map/all_gather | solution.py:78
  359.8 2.2 convolution_convert_fusion.1
  362.1 0.2 copy.29
  362.2 1.4 multiply_reduce_fusion
  363.6 0.0 copy-start
  363.6 1.8 fusion
  365.5 0.0 copy-done
  365.5 2.0 fusion.21
  367.5 293.7 %all-gather.8.cloned.1.call-done = bf16[1024,1024]{1,0:T(8,128)(2,1)} async-done(((bf16[16,1024]{1,0:T(8,128)(2,1)}), bf16[1024,1024]{1,0:T(8,128)(2,1)}) %all-gather.8.cloned.1.call-update) | async-done | bytes 2097168 | tf_op jit(solution)/shard_map/all_gather | solution.py:105
  661.2 2.8 fusion.17
  (3 shorter events, 0.0 us)
Async XLA Ops:
  6.5 49.7 %all-gather.4.cloned.1.call-start = ((), (), s32[]{:S(2)}) async-start(), calls=%async_computation.1 | async-start | bytes 2359296 | tf_op jit(solution)/shard_map/all_gather | solution.py:87
  7.3 352.6 %all-gather.6.cloned.1.call-start = ((), (), s32[]{:S(2)}) async-start(), calls=%async_computation.2 | async-start | bytes 2129920 | tf_op jit(solution)/shard_map/all_gather | solution.py:78
  12.0 58.8 %all-to-all-start = ((bf16[1,8,32,1024]{3,2,0,1:T(8,128)(2,1)}), bf16[1,8,32,1024]{3,2,0,1:T(8,128)(2,1)S(1)}, u32[]{:S(2)}, u32[]{:S(2)}) async-start(bf16[1,8,32,1024]{3,2,0,1:T(8,128)(2,1)} %fusion.15), calls=%async_computation | async-start | bytes 1048576 | tf_op jit(solution)/shard_map/all_to_all | solution.py:62
  22.3 638.9 %all-gather.8.cloned.1.call-start = ((), (), s32[]{:S(2)}) async-start(), calls=%async_computation.3 | async-start | bytes 2129920 | tf_op jit(solution)/shard_map/all_gather | solution.py:105
  363.6 1.8 copy-start
Sparse Core Ops, SparseCore 0:
  9.5 46.6 all-gather.3
  58.3 301.5 all-gather.5
  361.9 299.2 all-gather.7
where the time goes:
time: 671 us; the launch traced here: 670 us
  waiting for transfers between devices  616 us (92%)
  matrix products  18.1 us (3%)
  between operations  13.9 us (2%)
  starting transfers between devices  10.4 us (2%)
  local copies, waits for them, and re-layouts  7.37 us (1%)
    all_gather x1, waiting for transfers between devices, local(): lax.all_gather(w_out, 'win', axis=0, tiled=True)  294 us
    all_gather x1, waiting for transfers between devices, local(): lax.all_gather(w_q, 'win', axis=0, tiled=True)  289 us
    all_gather x1, waiting for transfers between devices, local(): lax.all_gather(frame_tokens, 'blk', axis=0, tiled=True)  30.7 us
  transfers between devices with their start and end apart: 4, of which 3 were waited for; matrix products, arithmetic and copies ran while one was open for 4% of the time, Pallas kernels for 0%

commit v1 on v0

--- a/solution.py
+++ b/solution.py
@@ -84,7 +84,9 @@
     )
     key_value = jnp.einsum(
         "fjpd,de->jfpe",
-        lax.all_gather(frame_tokens, "blk", axis=0, tiled=True),
+        jnp.concatenate(
+            lax.all_to_all(jnp.stack([frame_tokens] * lax.axis_size("blk")), "blk", 0, 0), axis=0
+        ),
         w_kv,
         preferred_element_type=jnp.float32,
     ).astype(jnp.bfloat16)

time: 671 us -> 635 us (0.946)
  waiting for transfers between devices: 616 us -> 577 us
    all_gather x1, waiting for transfers between devices: 289 us -> 216 us  [local(): lax.all_gather(w_q, 'win', axis=0, tiled=True)]
    all_to_all x0 -> x1, waiting for transfers between devices: none -> 55 us  [local(): lax.all_to_all(jnp.stack([frame_tokens] * lax.axis_size('blk')), 'blk', 0...]
    all_gather x1 -> x0, waiting for transfers between devices: 30.7 us -> none  [local(): lax.all_gather(frame_tokens, 'blk', axis=0, tiled=True)]
    all_to_all x0 -> x1, starting transfers between devices: none -> 10.3 us  [local(): lax.all_to_all(jnp.stack([frame_tokens] * lax.axis_size('blk')), 'blk', 0...]
    all_to_all x1, starting transfers between devices: 10.3 us -> 3.49 us  [local(): lax.all_to_all(outgoing, 'blk', split_axis=1, concat_axis=1, tiled=True)]
  transfers between devices with their start and end apart: 4 -> 4, of which waited for: 3 -> 4; matrix products, arithmetic and copies ran while one was open for 4% -> 4% of each run, Pallas kernels for 0% -> 0%
where the time goes in v1:
time: 635 us; the launch traced here: 634 us
  waiting for transfers between devices  577 us (91%)
  matrix products  16.7 us (3%)
  between operations  14.2 us (2%)
  starting transfers between devices  13.8 us (2%)
  local copies, waits for them, and re-layouts  9.9 us (2%)
    all_gather x1, waiting for transfers between devices, local(): lax.all_gather(w_out, 'win', axis=0, tiled=True)  300 us
    all_gather x1, waiting for transfers between devices, local(): lax.all_gather(w_q, 'win', axis=0, tiled=True)  216 us
    all_to_all x1, waiting for transfers between devices, local(): lax.all_to_all(jnp.stack([frame_tokens] * lax.axis_size('blk')), 'blk', 0...  55 us
  transfers between devices with their start and end apart: 4, of which 4 were waited for; matrix products, arithmetic and copies ran while one was open for 4% of the time, Pallas kernels for 0%

profile of v1, /device:TPU:8, one launch (start us, length us, event | category | flops | bytes accessed | tf_op | source)
XLA Modules:
  0.0 634.2 jit_solution(5890383572439869402)
XLA Ops:
  6.5 0.0 copy-start.1
  6.5 0.0 copy-start.2
  6.5 0.0 all-gather.3.cloned.1.call-start
  6.5 0.7 all-gather.3.cloned.1.call-update
  7.3 2.5 stack.2
  9.8 10.3 %all-to-all-start = ((bf16[8,1,1,128,1024]{4,3,2,1,0:T(8,128)(2,1)}), bf16[8,1,1,128,1024]{4,3,2,1,0:T(8,128)(2,1)S(1)}, u32[]{:S(2)}, u32[]{:S(2)}) async-start(bf16[8,1,1,128,1024]{4,3,2,1,0:T(8,128)(2,1)} %stack.2), calls=%async_computation | async-start | bytes 4194304 | tf_op jit(solution)/shard_map/all_to_all | solution.py:88
  20.1 0.0 all-gather.5.cloned.1.call-start
  20.1 0.7 all-gather.5.cloned.1.call-update
  20.9 0.0 copy-done.2
  20.9 0.1 fusion.34
  21.0 0.2 reduce_window_sum.22
  21.8 0.2 select_reduce_fusion
  22.0 0.3 reduce_window_sum.23
  22.3 0.0 copy-done.1
  22.3 1.4 fusion.15
  23.7 55.0 %all-to-all-done = bf16[8,1,1,128,1024]{4,3,2,1,0:T(8,128)(2,1)S(1)} async-done(((bf16[8,1,1,128,1024]{4,3,2,1,0:T(8,128)(2,1)}), bf16[8,1,1,128,1024]{4,3,2,1,0:T(8,128)(2,1)S(1)}, u32[]{:S(2)}, u32[]{:S(2)}) %all-to-all-start) | async-done | bytes 2097184 | tf_op jit(solution)/shard_map/all_to_all | solution.py:88
  78.7 3.5 all-to-all-start.1
  82.2 6.9 %fusion.8 = bf16[2048,8,128]{0,2,1:T(8,128)(2,1)S(1)} fusion(bf16[1024,2048]{1,0:T(8,128)(2,1)} %param.7, bf16[8,1,1,128,1024]{4,3,2,1,0:T(8,128)(2,1)S(1)} %all-to-all-done), kind=kOutput, calls=%fused_computation.9 | convolution fusion | flops 4297064448 | bytes 10485760 | tf_op jit(solution)/shard_map/fjpd,de->jfpe/dot_general | solution.py:85
  89.1 1.8 fusion.41
  90.9 2.6 copy.21
  93.4 2.9 copy.28
  96.3 4.2 all-to-all-done.1
  100.5 216.3 %all-gather.3.cloned.1.call-done = bf16[1024,1024]{1,0:T(8,128)(2,1)} async-done(((bf16[16,1024]{1,0:T(8,128)(2,1)}), bf16[1024,1024]{1,0:T(8,128)(2,1)}) %all-gather.3.cloned.1.call-update) | async-done | bytes 2097168 | tf_op jit(solution)/shard_map/all_gather | solution.py:78
  316.8 2.2 convolution_convert_fusion.1
  319.0 0.2 copy.27
  319.2 1.4 multiply_reduce_fusion
  320.6 0.0 copy-start
  320.6 1.8 fusion
  322.4 0.0 copy-done
  322.4 2.0 fusion.21
  324.4 300.2 %all-gather.5.cloned.1.call-done = bf16[1024,1024]{1,0:T(8,128)(2,1)} async-done(((bf16[16,1024]{1,0:T(8,128)(2,1)}), bf16[1024,1024]{1,0:T(8,128)(2,1)}) %all-gather.5.cloned.1.call-update) | async-done | bytes 2097168 | tf_op jit(solution)/shard_map/all_gather | solution.py:107
  624.6 2.8 fusion.17
  (7 shorter events, 0.1 us)
Async XLA Ops:
  6.5 15.8 %copy-start.1 = (bf16[1,1,128,1024]{3,2,1,0:T(8,128)(2,1)S(1)}, bf16[1,1,128,1024]{3,2,1,0:T(8,128)(2,1)}, u32[]{:S(2)}) copy-start(bf16[1,1,128,1024]{3,2,1,0:T(8,128)(2,1)} %param.6) | copy-start | bytes 786436
  6.5 14.3 %copy-start.2 = (s32[8,1,128]{2,1,0:T(1,128)S(1)}, s32[8,1,128]{2,1,0:T(1,128)}, u32[]{:S(2)}) copy-start(s32[8,1,128]{2,1,0:T(1,128)} %param.10) | copy-start | bytes 12292
  6.5 310.2 %all-gather.3.cloned.1.call-start = ((), (), s32[]{:S(2)}) async-start(), calls=%async_computation.2 | async-start | bytes 2129920 | tf_op jit(solution)/shard_map/all_gather | solution.py:78
  9.8 68.9 %all-to-all-start = ((bf16[8,1,1,128,1024]{4,3,2,1,0:T(8,128)(2,1)}), bf16[8,1,1,128,1024]{4,3,2,1,0:T(8,128)(2,1)S(1)}, u32[]{:S(2)}, u32[]{:S(2)}) async-start(bf16[8,1,1,128,1024]{4,3,2,1,0:T(8,128)(2,1)} %stack.2), calls=%async_computation | async-start | bytes 4194304 | tf_op jit(solution)/shard_map/all_to_all | solution.py:88
  20.1 604.5 %all-gather.5.cloned.1.call-start = ((), (), s32[]{:S(2)}) async-start(), calls=%async_computation.3 | async-start | bytes 2129920 | tf_op jit(solution)/shard_map/all_gather | solution.py:107
  78.7 21.8 %all-to-all-start.1 = ((bf16[1,8,32,1024]{3,2,0,1:T(8,128)(2,1)}), bf16[1,8,32,1024]{3,2,0,1:T(8,128)(2,1)S(1)}, u32[]{:S(2)}, u32[]{:S(2)}) async-start(bf16[1,8,32,1024]{3,2,0,1:T(8,128)(2,1)} %fusion.15), calls=%async_computation.1 | async-start | bytes 1048576 | tf_op jit(solution)/shard_map/all_to_all | solution.py:62
  320.6 1.8 copy-start
Sparse Core Ops, SparseCore 0:
  9.4 307.2 all-gather.2
  318.9 305.6 all-gather.4
